TPU v7x, 32 devices: a whole 2x2x4 slice. The times are simulated.
32 devices in a mesh: dp: 8 (over z, core), sp: 4 (over y, x).
Axes of the slice: x: 2, y: 2, z: 4, core: 2. Of those that a mesh axis runs over, the one named last changes fastest.
Arguments:
- gate_pre: bfloat16 [2048, 8192], P('dp', 'sp'), may hold values from -6 to 6
- up_pre: bfloat16 [2048, 8192], P('dp', 'sp'), may hold values from -6 to 6
- w_down: bfloat16 [8192, 6144], P('sp'), may hold values from -0.0625 to 0.0625
- route_logits: float32 [4096, 2], P(('dp', 'sp')), may hold values from -8 to 8
- expert_ids: int32 [4096, 2], P(('dp', 'sp')), may hold values from 0 to 7, as said below
- d_out: bfloat16 [4096, 6144], P(('dp', 'sp')), may hold values from -6 to 6
Outputs:
- mixed: bfloat16 [4096, 6144], P(('dp', 'sp'))
- logit_grads: float32 [4096, 2], P(('dp', 'sp'))
- gate_grads: bfloat16 [2048, 8192], P('dp', 'sp')
- up_grads: bfloat16 [2048, 8192], P('dp', 'sp')
- down_grads: float32 [8192, 6144], P('sp', 'dp')
Inputs may be any that keep to these rules, and one draw needn't show every extreme that they name: `expert_ids`: each row names two different experts. Of the 128 rows of one device, a quarter of 64 up to 64 name expert 0, and exactly 64 on some device in every draw.
All inputs are finite; a program needn't handle non-finite values.
Results may differ from a plain program's by a relative error of at most 0.022.
Values may be sent and summed in bfloat16 or wider, within the bound.
A program may use at most 128 MiB of HBM per device.

v0:
```python
import jax
import jax.numpy as jnp
from jax import lax
from jax.sharding import PartitionSpec as P


def contract_rows(left, right):
    return lax.dot_general(
        left, right, (((0,), (0,)), ((), ())), preferred_element_type=jnp.float32
    )


def contract_cols(left, right):
    return lax.dot_general(
        left, right, (((1,), (1,)), ((), ())), preferred_element_type=jnp.float32
    )


def plain_product(left, right):
    return jnp.dot(left, right, preferred_element_type=jnp.float32)


def local(gate_pre, up_pre, w_down, route_logits, expert_ids, d_out):
    tok_rows = expert_ids.shape[0]
    slot_rows = tok_rows // 2
    routed = jnp.any(expert_ids == 0, axis=1)
    routed_int = routed.astype(jnp.int32)
    routed_float = routed.astype(jnp.float32)
    slot_rank = jnp.cumsum(routed_int) - 1
    gate_wide = gate_pre.astype(jnp.float32)
    up_wide = up_pre.astype(jnp.float32)
    sigma_gate = jax.nn.sigmoid(gate_wide)
    silu_gate = gate_wide * sigma_gate
    hidden = (silu_gate * up_wide).astype(jnp.bfloat16)
    expert_out = lax.psum_scatter(
        plain_product(hidden, w_down).astype(jnp.bfloat16), "sp", scatter_dimension=0, tiled=True
    ).astype(jnp.float32)
    safe_rank = jnp.clip(slot_rank, 0, slot_rows - 1)
    token_out = expert_out[safe_rank] * routed_float[:, None]
    first_zero = expert_ids[:, 0] == 0
    own_logit = jnp.where(first_zero, route_logits[:, 0], route_logits[:, 1])
    other_logit = jnp.where(first_zero, route_logits[:, 1], route_logits[:, 0])
    weight_zero = routed_float * jax.nn.sigmoid(own_logit - other_logit)
    mixed = (weight_zero[:, None] * token_out).astype(jnp.bfloat16)
    weight_grad = jnp.sum(d_out.astype(jnp.float32) * token_out, axis=1)
    logit_grad = weight_grad * weight_zero * (1.0 - weight_zero)
    first_col = jnp.where(first_zero, logit_grad, -logit_grad)
    logit_grads = jnp.stack([first_col, -first_col], axis=1)
    chooser = (slot_rank[:, None] == jnp.arange(slot_rows, dtype=jnp.int32)[None, :]) & routed[
        :, None
    ]
    picked = contract_rows(chooser.astype(jnp.bfloat16), d_out)
    slot_weight = lax.dot_general(
        chooser.astype(jnp.float32),
        weight_zero,
        (((0,), (0,)), ((), ())),
        precision=lax.Precision.HIGHEST,
        preferred_element_type=jnp.float32,
    )
    d_expert = (slot_weight[:, None] * picked).astype(jnp.bfloat16)
    piece = lax.all_gather(d_expert, "sp", axis=0, tiled=True)
    part_hidden = contract_cols(piece, w_down)
    d_hidden = part_hidden
    extra_part = piece
    d_hidden, extra_part = (d_hidden, extra_part)
    cycle_blocks = lax.all_to_all(extra_part, "dp", split_axis=1, concat_axis=0, tiled=True)
    down_grads = contract_rows(lax.all_gather(hidden, "dp", axis=0, tiled=True), cycle_blocks)
    gate_grads = (d_hidden * up_wide * sigma_gate * (1.0 + gate_wide * (1.0 - sigma_gate))).astype(
        jnp.bfloat16
    )
    up_grads = (d_hidden * silu_gate).astype(jnp.bfloat16)
    return (mixed, logit_grads, gate_grads, up_grads, down_grads)


def solution(mesh):
    return jax.shard_map(
        local,
        mesh=mesh,
        in_specs=(
            P("dp", "sp"),
            P("dp", "sp"),
            P("sp", None),
            P(("dp", "sp"), None),
            P(("dp", "sp"), None),
            P(("dp", "sp"), None),
        ),
        out_specs=(
            P(("dp", "sp"), None),
            P(("dp", "sp"), None),
            P("dp", "sp"),
            P("dp", "sp"),
            P("sp", "dp"),
        ),
        check_vma=False,
    )
```

profile of v0, /device:TPU:0, one launch (start us, length us, event | category | flops | bytes accessed | tf_op | source)
XLA Modules:
  0.0 289.5 jit_solution(3769832607676820949)
XLA Ops:
  7.2 0.0 reduce-scatter.2.cloned.1.call-start
  7.2 2.2 fusion.1
  9.4 0.0 copy-start.2
  9.4 13.1 %convolution_convert_fusion = bf16[256,6144]{1,0:T(8,128)(2,1)} fusion(bf16[256,2048]{1,0:T(8,128)(2,1)S(1)} %fusion.1, bf16[2048,6144]{1,0:T(8,128)(2,1)} %param.8), kind=kOutput, calls=%fused_computation.1 | convolution fusion | flops 6444023808 | bytes 29360128 | tf_op jit(solution)/shard_map/dot_general | solution.py:20
  22.5 0.0 copy-done.2
  22.5 0.0 copy-start.4
  22.5 0.0 reduce-scatter.2.cloned.1.call-update
  22.6 0.0 all-gather.3.cloned.1.call-start
  22.6 0.6 copy-done.4
  23.3 0.1 copy.50
  23.4 0.2 reduce-window.4
  23.5 0.1 copy.51
  23.6 45.7 %reduce-scatter.2.cloned.1.call-done = bf16[64,6144]{1,0:T(8,128)(2,1)} async-done(((bf16[256,6144]{1,0:T(8,128)(2,1)}), bf16[64,6144]{1,0:T(8,128)(2,1)}) %reduce-scatter.2.cloned.1.call-update) | async-done | bytes 786448 | tf_op jit(solution)/shard_map/reduce_scatter | solution.py:35
  69.3 1.2 convert_element_type.53
  70.6 0.0 copy-start.1
  70.6 3.2 %gather_fusion = f32[128,6144]{1,0:T(8,128)} fusion(f32[64,6144]{1,0:T(8,128)S(1)} %convert_element_type.53, s32[1024]{0:T(1024)S(1)} %pad_clamp_fusion), kind=kCustom, calls=%fused_computation | custom fusion | bytes 6291968 | tf_op jit(solution)/shard_map/gather | solution.py:39
  73.8 0.0 copy-start.3
  73.8 0.0 copy-done.1
  73.8 2.5 multiply_reduce_fusion
  76.3 0.0 copy-done.3
  76.3 0.2 convolution_bitcast_fusion
  76.5 1.4 fusion
  77.9 0.0 all-gather.3.cloned.1.call-update
  77.9 0.0 all-gather.5.cloned.1.call-start
  78.0 0.7 all-gather.5.cloned.1.call-update
  78.7 43.3 %all-gather.3.cloned.1.call-done = bf16[256,6144]{1,0:T(8,128)(2,1)} async-done(((bf16[64,6144]{1,0:T(8,128)(2,1)}), bf16[256,6144]{1,0:T(8,128)(2,1)}) %all-gather.3.cloned.1.call-update) | async-done | bytes 3145744 | tf_op jit(solution)/shard_map/all_gather | solution.py:61
  121.9 3.7 %copy.55 = bf16[32,8,8,768]{3,2,0,1:T(8,128)(2,1)} copy(bf16[32,8,8,768]{3,2,1,0:T(8,128)(2,1)} %bitcast.46) | data formatting | bytes 6291456 | tf_op jit(solution)/shard_map/all_to_all | solution.py:66
  125.6 0.0 copy-start
  125.6 4.9 %all-to-all-start = ((bf16[256,8,768]{2,0,1:T(8,128)(2,1)}), bf16[256,8,768]{2,0,1:T(8,128)(2,1)}, u32[]{:S(2)}, u32[]{:S(2)}) async-start(bf16[256,8,768]{2,0,1:T(8,128)(2,1)} %bitcast.45), calls=%async_computation.1 | async-start | bytes 6291456 | tf_op jit(solution)/shard_map/all_to_all | solution.py:66
  130.6 0.6 pad_maximum_fusion
  131.1 0.0 copy-done
  131.1 1.6 multiply_convert_fusion
  132.7 14.7 %multiply_convert_fusion.1 = (bf16[256,2048]{1,0:T(8,128)(2,1)}, bf16[256,2048]{1,0:T(8,128)(2,1)}) fusion(bf16[256,2048]{1,0:T(8,128)(2,1)} %param.6, bf16[256,2048]{1,0:T(8,128)(2,1)} %param.7, bf16[256,6144]{1,0:T(8,128)(2,1)} %all-gather.3.cloned.1.call-done, bf16[2048,6144]{1,0:T(8,128)(2,1)} %param.8), kind=kOutput, calls=%fused_computation.20 | convolution fusion | flops 6450315264 | bytes 32505856 | tf_op jit(solution)/shard_map/dot_general | solution.py:14
  147.4 123.7 %all-gather.5.cloned.1.call-done = bf16[2048,2048]{1,0:T(8,128)(2,1)} async-done(((bf16[256,2048]{1,0:T(8,128)(2,1)}), bf16[2048,2048]{1,0:T(8,128)(2,1)}) %all-gather.5.cloned.1.call-update) | async-done | bytes 8388624 | tf_op jit(solution)/shard_map/all_gather | solution.py:67
  271.1 0.0 all-to-all-done
  271.1 11.9 %fusion.24 = f32[2048,768]{1,0:T(8,128)} fusion(bf16[2048,2048]{1,0:T(8,128)(2,1)} %all-gather.5.cloned.1.call-done, bf16[2048,768]{1,0:T(8,128)(2,1)} %bitcast.9), kind=kOutput, calls=%fused_computation.47 | convolution fusion | flops 6442450944 | bytes 17825792 | tf_op jit(solution)/shard_map/dot_general | solution.py:8
  (6 shorter events, 0.1 us)
Async XLA Ops:
  7.2 62.2 %reduce-scatter.2.cloned.1.call-start = ((), (), s32[]{:S(2)}) async-start(), calls=%async_computation.2 | async-start | bytes 3932160 | tf_op jit(solution)/shard_map/reduce_scatter | solution.py:35
  9.4 13.1 %copy-start.2 = (bf16[256,2048]{1,0:T(8,128)(2,1)}, bf16[256,2048]{1,0:T(8,128)(2,1)S(1)}, u32[]{:S(2)}) copy-start(bf16[256,2048]{1,0:T(8,128)(2,1)S(1)} %fusion.1) | copy-start | bytes 3145732
  22.5 0.7 copy-start.4
  22.6 99.4 %all-gather.3.cloned.1.call-start = ((), (), s32[]{:S(2)}) async-start(), calls=%async_computation.3 | async-start | bytes 3932160 | tf_op jit(solution)/shard_map/all_gather | solution.py:61
  70.6 3.2 %copy-start.1 = (bf16[128,6144]{1,0:T(8,128)(2,1)S(1)}, bf16[128,6144]{1,0:T(8,128)(2,1)}, u32[]{:S(2)}) copy-start(bf16[128,6144]{1,0:T(8,128)(2,1)} %param.11) | copy-start | bytes 4718596
  73.8 2.5 copy-start.3
  77.9 193.2 %all-gather.5.cloned.1.call-start = ((), (), s32[]{:S(2)}) async-start(), calls=%async_computation.4 | async-start | bytes 9437184 | tf_op jit(solution)/shard_map/all_gather | solution.py:67
  125.6 5.5 %copy-start = (f32[128,6144]{1,0:T(8,128)S(1)}, f32[128,6144]{1,0:T(8,128)}, u32[]{:S(2)}) copy-start(f32[128,6144]{1,0:T(8,128)} %gather_fusion) | copy-start | bytes 9437188
  125.6 145.4 %all-to-all-start = ((bf16[256,8,768]{2,0,1:T(8,128)(2,1)}), bf16[256,8,768]{2,0,1:T(8,128)(2,1)}, u32[]{:S(2)}, u32[]{:S(2)}) async-start(bf16[256,8,768]{2,0,1:T(8,128)(2,1)} %bitcast.45), calls=%async_computation.1 | async-start | bytes 6291456 | tf_op jit(solution)/shard_map/all_to_all | solution.py:66
Sparse Core Ops, SparseCore 0:
  22.7 46.6 reduce-scatter.1
  78.0 43.8 all-gather.2
  123.5 147.4 all-gather.4
where the time goes:
time: 290 us; the launch traced here: 289 us
  waiting for transfers between devices  213 us (73%)
  matrix products  41.3 us (14%)
  between operations  13.8 us (5%)
  other arithmetic  8.3 us (3%)
  local copies, waits for them, and re-layouts  7.69 us (3%)
  starting transfers between devices  5.04 us (2%)
    all_gather x1, waiting for transfers between devices, local(): lax.all_gather(hidden, 'dp', axis=0, tiled=True)  124 us
    reduce_scatter x1, waiting for transfers between devices, local(): lax.psum_scatter(plain_product(hidden, w_down).astype(jnp.bfloat16), 'sp'...  45.7 us
    all_gather x1, waiting for transfers between devices, local(): piece = lax.all_gather(d_expert, 'sp', axis=0, tiled=True)  43.3 us
    dot_general x1, matrix products, contract_cols(): lax.dot_general(left, right, (((1,), (1,)), ((), ())), preferred_element_...  14.7 us
    dot_general x2, matrix products, contract_rows(): lax.dot_general(left, right, (((0,), (0,)), ((), ())), preferred_element_...  13.3 us
    dot_general x1, matrix products, plain_product(): return jnp.dot(left, right, preferred_element_type=jnp.float32)  13.1 us
  transfers between devices with their start and end apart: 4, of which 3 were waited for; matrix products, arithmetic and copies ran while one was open for 7% of the time, Pallas kernels for 0%

commit v1 on v0

--- a/solution.py
+++ b/solution.py
@@ -2,6 +2,16 @@
 import jax.numpy as jnp
 from jax import lax
 from jax.sharding import PartitionSpec as P
+
+
+def gather_by_hops(block, mesh_axis, dim):
+    size = lax.axis_size(mesh_axis)
+    held, tiles = (block, [block])
+    for _ in range(size - 1):
+        held = lax.ppermute(held, mesh_axis, [(i, (i + 1) % size) for i in range(size)])
+        tiles.insert(0, held)
+    flat = jnp.concatenate(tiles, axis=dim)
+    return jnp.roll(flat, (lax.axis_index(mesh_axis) + 1) * block.shape[dim], axis=dim)
 
 
 def contract_rows(left, right):
@@ -58,7 +68,7 @@
         preferred_element_type=jnp.float32,
     )
     d_expert = (slot_weight[:, None] * picked).astype(jnp.bfloat16)
-    piece = lax.all_gather(d_expert, "sp", axis=0, tiled=True)
+    piece = gather_by_hops(d_expert, "sp", 0)
     part_hidden = contract_cols(piece, w_down)
     d_hidden = part_hidden
     extra_part = piece

time: 290 us -> 238 us (0.82)
  waiting for transfers between devices: 213 us -> 157 us
    all_gather x1, waiting for transfers between devices: 124 us -> 0.03 us  [local(): lax.all_gather(hidden, 'dp', axis=0, tiled=True)]
    ppermute x0 -> x3, waiting for transfers between devices: none -> 55.8 us  [gather_by_hops(): lax.ppermute(held, mesh_axis, [(i, (i + 1) % size) for i in range(size)])]
    all_to_all x1, waiting for transfers between devices: 0.01 us -> 54.9 us  [local(): lax.all_to_all(extra_part, 'dp', split_axis=1, concat_axis=0, tiled=True)]
    all_gather x1 -> x0, waiting for transfers between devices: 43.3 us -> none  [local(): piece = lax.all_gather(d_expert, 'sp', axis=0, tiled=True)]
    dynamic_slice x0 -> x2, local copies, waits for them, and re-layouts: none -> 3.45 us  [gather_by_hops(): jnp.roll(flat, (lax.axis_index(mesh_axis) + 1) * block.shape[dim], axis=dim)]
  transfers between devices with their start and end apart: 4 -> 6, of which waited for: 3 -> 5; matrix products, arithmetic and copies ran while one was open for 7% -> 13% of each run, Pallas kernels for 0% -> 0%
where the time goes in v1:
time: 238 us
  waiting for transfers between devices  157 us (66%)
  matrix products  39.2 us (16%)
  between operations  15.6 us (7%)
  local copies, waits for them, and re-layouts  10.5 us (4%)
  other arithmetic  8.33 us (4%)
  starting transfers between devices  7.11 us (3%)
    ppermute x3, waiting for transfers between devices, gather_by_hops(): lax.ppermute(held, mesh_axis, [(i, (i + 1) % size) for i in range(size)])  55.8 us
    all_to_all x1, waiting for transfers between devices, local(): lax.all_to_all(extra_part, 'dp', split_axis=1, concat_axis=0, tiled=True)  54.9 us
    reduce_scatter x1, waiting for transfers between devices, local(): lax.psum_scatter(plain_product(hidden, w_down).astype(jnp.bfloat16), 'sp'...  45.7 us
    dot_general x1, matrix products, contract_cols(): lax.dot_general(left, right, (((1,), (1,)), ((), ())), preferred_element_...  14.5 us
    dot_general x1, matrix products, plain_product(): return jnp.dot(left, right, preferred_element_type=jnp.float32)  13.1 us
    dot_general x2, matrix products, contract_rows(): lax.dot_general(left, right, (((0,), (0,)), ((), ())), preferred_element_...  11.4 us
    all_to_all x1, starting transfers between devices, local(): lax.all_to_all(extra_part, 'dp', split_axis=1, concat_axis=0, tiled=True)  4.93 us
  transfers between devices with their start and end apart: 6, of which 5 were waited for; matrix products, arithmetic and copies ran while one was open for 13% of the time, Pallas kernels for 0%

profile of v1, /device:TPU:0, one launch (start us, length us, event | category | flops | bytes accessed | tf_op | source)
XLA Modules:
  0.0 237.8 jit_solution(6880707699554246688)
XLA Ops:
  8.0 0.0 reduce-scatter.2.cloned.1.call-start
  8.0 2.2 fusion.1
  10.3 0.0 copy-start.3
  10.3 13.1 %convolution_convert_fusion = bf16[256,6144]{1,0:T(8,128)(2,1)} fusion(bf16[256,2048]{1,0:T(8,128)(2,1)S(1)} %fusion.1, bf16[2048,6144]{1,0:T(8,128)(2,1)} %param.8), kind=kOutput, calls=%fused_computation.1 | convolution fusion | flops 6444023808 | bytes 29360128 | tf_op jit(solution)/shard_map/dot_general | solution.py:30
  23.4 0.0 copy-done.3
  23.4 0.0 reduce-scatter.2.cloned.1.call-update
  23.4 0.0 all-gather.2.cloned.1.call-start
  23.5 0.5 all-gather.2.cloned.1.call-update
  24.0 0.1 copy-done.5
  24.1 0.1 copy.64
  24.2 0.2 reduce-window.4
  24.4 0.1 copy.65
  24.5 45.7 %reduce-scatter.2.cloned.1.call-done = bf16[64,6144]{1,0:T(8,128)(2,1)} async-done(((bf16[256,6144]{1,0:T(8,128)(2,1)}), bf16[64,6144]{1,0:T(8,128)(2,1)}) %reduce-scatter.2.cloned.1.call-update) | async-done | bytes 786448 | tf_op jit(solution)/shard_map/reduce_scatter | solution.py:45
  70.2 1.3 convert_element_type.53
  71.4 0.0 copy-start.2
  71.5 3.2 %gather_fusion = f32[128,6144]{1,0:T(8,128)} fusion(f32[64,6144]{1,0:T(8,128)S(1)} %convert_element_type.53, s32[1024]{0:T(1024)S(1)} %pad_clamp_fusion), kind=kCustom, calls=%fused_computation | custom fusion | bytes 6291968 | tf_op jit(solution)/shard_map/gather | solution.py:49
  74.6 0.0 copy-done.2
  74.6 2.5 %multiply_reduce_fusion = f32[128]{0:T(128)S(1)} fusion(bf16[128,6144]{1,0:T(8,128)(2,1)S(1)} %copy-done.2, f32[128,6144]{1,0:T(8,128)} %gather_fusion, f32[128]{0:T(128)S(1)} %get-tuple-element.27), kind=kLoop, calls=%fused_computation.4 | loop fusion | flops 3145600 | bytes 4719616 | tf_op jit(solution)/shard_map/reduce_sum | solution.py:55
  77.1 0.0 copy-done.4
  77.1 0.2 convolution_bitcast_fusion
  77.4 0.5 fusion
  77.9 1.5 collective-permute-start
  79.4 18.6 %collective-permute-done = bf16[64,6144]{1,0:T(8,128)(2,1)S(1)} collective-permute-done((bf16[64,6144]{1,0:T(8,128)(2,1)S(1)}, bf16[64,6144]{1,0:T(8,128)(2,1)S(1)}, u32[]{:S(2)}, u32[]{:S(2)}) %collective-permute-start) | collective-permute-done | bytes 786464 | tf_op jit(solution)/shard_map/ppermute | solution.py:11
  98.0 0.6 collective-permute-start.1
  98.6 18.7 %collective-permute-done.1 = bf16[64,6144]{1,0:T(8,128)(2,1)S(1)} collective-permute-done((bf16[64,6144]{1,0:T(8,128)(2,1)S(1)}, bf16[64,6144]{1,0:T(8,128)(2,1)S(1)}, u32[]{:S(2)}, u32[]{:S(2)}) %collective-permute-start.1) | collective-permute-done | bytes 786464 | tf_op jit(solution)/shard_map/ppermute | solution.py:11
  117.3 0.0 collective-permute-start.2
  117.3 18.5 %collective-permute-done.2 = bf16[64,6144]{1,0:T(8,128)(2,1)S(1)} collective-permute-done((bf16[64,6144]{1,0:T(8,128)(2,1)S(1)}, bf16[64,6144]{1,0:T(8,128)(2,1)S(1)}, u32[]{:S(2)}, u32[]{:S(2)}) %collective-permute-start.2) | collective-permute-done | bytes 786464 | tf_op jit(solution)/shard_map/ppermute | solution.py:11
  135.8 0.1 constant_dynamic-update-slice_fusion.7
  135.8 0.1 constant_dynamic-update-slice_fusion.6
  135.9 0.1 constant_dynamic-update-slice_fusion.5
  135.9 0.1 constant_dynamic-update-slice_fusion.4
  136.0 0.1 constant_dynamic-update-slice_fusion.3
  136.1 0.1 constant_dynamic-update-slice_fusion.2
  136.1 0.1 constant_dynamic-update-slice_fusion.1
  136.2 0.1 constant_dynamic-update-slice_fusion
  136.3 0.2 constant_dynamic-slice_fusion
  136.5 0.0 copy-start.1
  136.5 3.2 %copy.66 = bf16[256,6144]{0,1:T(8,128)(2,1)} copy(bf16[256,6144]{1,0:T(8,128)(2,1)S(1)} %constant_dynamic-slice_fusion) | data formatting | bytes 6291456 | tf_op jit(solution)/shard_map/jit(_roll_dynamic)/dynamic_slice | solution.py:14
  139.7 0.0 copy-done.1
  139.7 4.9 %all-to-all-start = ((bf16[256,8,768]{0,2,1:T(8,128)(2,1)}), bf16[256,8,768]{0,2,1:T(8,128)(2,1)}, u32[]{:S(2)}, u32[]{:S(2)}) async-start(bf16[256,8,768]{0,2,1:T(8,128)(2,1)} %bitcast.41), calls=%async_computation.1 | async-start | bytes 6291456 | tf_op jit(solution)/shard_map/all_to_all | solution.py:76
  144.7 0.6 pad_maximum_fusion
  145.2 0.0 copy-done
  145.2 1.6 multiply_convert_fusion
  146.8 14.5 %multiply_convert_fusion.1 = (bf16[256,2048]{1,0:T(8,128)(2,1)}, bf16[256,2048]{1,0:T(8,128)(2,1)}) fusion(bf16[256,2048]{1,0:T(8,128)(2,1)} %param.6, bf16[256,2048]{1,0:T(8,128)(2,1)} %param.7, bf16[256,6144]{1,0:T(8,128)(2,1)} %copy-done.1, bf16[2048,6144]{1,0:T(8,128)(2,1)} %param.8), kind=kOutput, calls=%fused_computation.19 | convolution fusion | flops 6450315264 | bytes 32505856 | tf_op jit(solution)/shard_map/dot_general | solution.py:24
  161.3 54.9 %all-to-all-done = bf16[256,8,768]{0,2,1:T(8,128)(2,1)} async-done(((bf16[256,8,768]{0,2,1:T(8,128)(2,1)}), bf16[256,8,768]{0,2,1:T(8,128)(2,1)}, u32[]{:S(2)}, u32[]{:S(2)}) %all-to-all-start) | async-done | bytes 3145760 | tf_op jit(solution)/shard_map/all_to_all | solution.py:76
  216.2 3.2 %copy.67 = bf16[8,256,768]{2,1,0:T(8,128)(2,1)S(1)} copy(bf16[8,256,768]{1,2,0:T(8,128)(2,1)} %bitcast.9) | data formatting | bytes 6291456 | tf_op jit(solution)/shard_map/all_to_all | solution.py:76
  219.4 0.0 all-gather.2.cloned.1.call-done
  219.5 10.9 %fusion.24 = f32[2048,768]{1,0:T(8,128)} fusion(bf16[2048,2048]{1,0:T(8,128)(2,1)} %all-gather.2.cloned.1.call-done, bf16[2048,768]{1,0:T(8,128)(2,1)S(1)} %bitcast.42), kind=kOutput, calls=%fused_computation.55 | convolution fusion | flops 6442450944 | bytes 17825792 | tf_op jit(solution)/shard_map/dot_general | solution.py:18
  (9 shorter events, 0.1 us)
Async XLA Ops:
  8.0 62.2 %reduce-scatter.2.cloned.1.call-start = ((), (), s32[]{:S(2)}) async-start(), calls=%async_computation.2 | async-start | bytes 3932160 | tf_op jit(solution)/shard_map/reduce_scatter | solution.py:45
  10.3 13.1 %copy-start.3 = (bf16[256,2048]{1,0:T(8,128)(2,1)}, bf16[256,2048]{1,0:T(8,128)(2,1)S(1)}, u32[]{:S(2)}) copy-start(bf16[256,2048]{1,0:T(8,128)(2,1)S(1)} %fusion.1) | copy-start | bytes 3145732
  23.4 0.7 copy-start.5
  23.4 196.0 %all-gather.2.cloned.1.call-start = ((), (), s32[]{:S(2)}) async-start(), calls=%async_computation.3 | async-start | bytes 9437184 | tf_op jit(solution)/shard_map/all_gather | solution.py:77
  71.4 3.2 %copy-start.2 = (bf16[128,6144]{1,0:T(8,128)(2,1)S(1)}, bf16[128,6144]{1,0:T(8,128)(2,1)}, u32[]{:S(2)}) copy-start(bf16[128,6144]{1,0:T(8,128)(2,1)} %param.11) | copy-start | bytes 4718596
  74.6 2.5 %copy-start.4 = (f32[128,2]{0,1:T(2,128)S(1)}, f32[128,2]{0,1:T(2,128)}, u32[]{:S(2)}) copy-start(f32[128,2]{0,1:T(2,128)} %param.9) | copy-start | bytes 3076
  77.9 20.1 %collective-permute-start = (bf16[64,6144]{1,0:T(8,128)(2,1)S(1)}, bf16[64,6144]{1,0:T(8,128)(2,1)S(1)}, u32[]{:S(2)}, u32[]{:S(2)}) collective-permute-start(bf16[64,6144]{1,0:T(8,128)(2,1)S(1)} %fusion), channel_id=1, source_target_pairs={{0,1},{1,2},{2,3},{3,0},{4,5},{5,6},{6,7},{7,4},{8,9},{9,10},{10,1... | collective-permute-start | bytes 2359304 | tf_op jit(solution)/shard_map/ppermute | solution.py:11
  98.0 19.3 %collective-permute-start.1 = (bf16[64,6144]{1,0:T(8,128)(2,1)S(1)}, bf16[64,6144]{1,0:T(8,128)(2,1)S(1)}, u32[]{:S(2)}, u32[]{:S(2)}) collective-permute-start(bf16[64,6144]{1,0:T(8,128)(2,1)S(1)} %collective-permute-done), channel_id=1, source_target_pairs={{0,1},{1,2},{2,3},{3,0},{4,5},{5,6},{6,7},{7,4},{8,9},{9,10},{10,1... | collective-permute-start | bytes 2359304 | tf_op jit(solution)/shard_map/ppermute | solution.py:11
  117.3 18.5 %collective-permute-start.2 = (bf16[64,6144]{1,0:T(8,128)(2,1)S(1)}, bf16[64,6144]{1,0:T(8,128)(2,1)S(1)}, u32[]{:S(2)}, u32[]{:S(2)}) collective-permute-start(bf16[64,6144]{1,0:T(8,128)(2,1)S(1)} %collective-permute-done.1), channel_id=1, source_target_pairs={{0,1},{1,2},{2,3},{3,0},{4,5},{5,6},{6,7},{7,4},{8,9},{9,10},{10,1... | collective-permute-start | bytes 2359304 | tf_op jit(solution)/shard_map/ppermute | solution.py:11
  136.5 3.2 %copy-start.1 = (bf16[256,6144]{1,0:T(8,128)(2,1)}, bf16[256,6144]{1,0:T(8,128)(2,1)S(1)}, u32[]{:S(2)}) copy-start(bf16[256,6144]{1,0:T(8,128)(2,1)S(1)} %constant_dynamic-slice_fusion) | copy-start | bytes 9437188
  139.7 5.5 %copy-start = (f32[128,6144]{1,0:T(8,128)S(1)}, f32[128,6144]{1,0:T(8,128)}, u32[]{:S(2)}) copy-start(f32[128,6144]{1,0:T(8,128)} %gather_fusion) | copy-start | bytes 9437188
  139.7 76.5 %all-to-all-start = ((bf16[256,8,768]{0,2,1:T(8,128)(2,1)}), bf16[256,8,768]{0,2,1:T(8,128)(2,1)}, u32[]{:S(2)}, u32[]{:S(2)}) async-start(bf16[256,8,768]{0,2,1:T(8,128)(2,1)} %bitcast.41), calls=%async_computation.1 | async-start | bytes 6291456 | tf_op jit(solution)/shard_map/all_to_all | solution.py:76
Sparse Core Ops, SparseCore 0:
  23.5 46.6 reduce-scatter.1
Sparse Core Ops, SparseCore 1:
  25.5 84.6 all-gather.1
